TPU v7x, 32 devices: a whole 2x2x4 slice. The times are simulated.
32 devices in a mesh: groups: 2 (over y), det: 4 (over z), blk: 2 (over x), sub: 2 (over core).
Axes of the slice: x: 2, y: 2, z: 4, core: 2. Of those that a mesh axis runs over, the one named last changes fastest.
Arguments:
- tod: float32 [256, 4, 1024], P(('groups', 'det'), None, ('blk', 'sub')), parts along dimension 0, may hold values from -30 to 30
- pixels: int32 [256, 4, 1024], P('groups', 'det', ('blk', 'sub')), parts along dimension 0, may hold values from 0 to 3071
- span_block: int32 [8, 8], P('groups', ('blk', 'sub')), parts along dimension 0, may hold values from 0 to 7
- weight_class: int32 [256], P('groups'), parts along dimension 0, may hold values from 0 to 7
- class_weight: float32 [16], P('groups'), parts along dimension 0, may hold values from 0.25 to 4
Outputs:
- signal_sum: float32 [16, 3072], P(('groups', 'blk'), ('det', 'sub')), parts along dimension 0
- weight_sum: float32 [16, 3072], P(('groups', 'blk'), ('det', 'sub')), parts along dimension 0
- hit_count: float32 [16, 3072], P(('groups', 'blk'), ('det', 'sub')), parts along dimension 0
There are 2 independent parts, one for each index of `groups`. A program takes and returns all parts, laid end to end along the dimension named above; each array names one. Nothing has to cross between parts.
All inputs are finite; a program needn't handle non-finite values.
Results may differ from a plain program's by a relative error of at most 0.005.
Values sent between devices are 32-bit elements; how exact they have to be, the bound alone decides.
No kernel may reach another device: no remote copies, remote signals or barrier semaphores. Data moves between devices by JAX's collectives and lax.ppermute only.
A program may use at most 64 MiB of HBM per device.

v0:
```python
import jax
import jax.numpy as jnp
from jax import lax
from jax.sharding import PartitionSpec as P

BLOCK_PIX = 3072
SPAN = 128
BLK_OWN = 4


def on_device(tod, pixels, span_block, weight_class, class_weight):
    classes = class_weight.shape[0]
    picker = (weight_class[:, None] == jnp.arange(classes, dtype=jnp.int32)[None, :]).astype(
        jnp.float32
    )
    weight = jnp.sum(picker * class_weight[None, :], axis=1)
    total = jnp.sum(weight)
    regrouped = lax.all_to_all(tod, "det", split_axis=1, concat_axis=0, tiled=True)
    common = jnp.sum(weight[:, None, None] * regrouped, axis=0, keepdims=True) / total
    values = (weight[:, None, None] * (regrouped - common)).astype(jnp.bfloat16)
    detectors = values.shape[0]
    samples = values.shape[2]
    spans = samples // SPAN
    groups = 4
    size_group = detectors // groups
    turns = groups * spans
    own_row = lax.dynamic_slice_in_dim(span_block, lax.axis_index("det"), 1, 0)[0]
    values = (
        values.reshape(groups, size_group, spans, SPAN)
        .transpose(0, 2, 1, 3)
        .reshape(turns, size_group, SPAN)
    )
    where = (
        pixels.reshape(groups, size_group, spans, SPAN)
        .transpose(0, 2, 1, 3)
        .reshape(turns, size_group, SPAN)
    )
    weight_low = weight.astype(jnp.bfloat16).reshape(groups, 1, size_group)
    weight_low = jnp.broadcast_to(weight_low, (groups, spans, size_group)).reshape(
        turns, size_group
    )
    span_of = jnp.broadcast_to(
        jnp.arange(spans, dtype=jnp.int32)[None, :], (groups, spans)
    ).reshape(turns)
    lanes = 128
    upper = BLOCK_PIX // lanes
    nblocks = BLK_OWN * lax.axis_size("blk")
    count = size_group * SPAN
    selector = (span_of[:, None] == jnp.arange(spans, dtype=jnp.int32)[None, :]).astype(jnp.float32)

    def bin_tile(total_map, item):
        tile_values, tile_pixels, tile_weight, select = item
        high = tile_pixels // lanes
        low = tile_pixels % lanes
        high_hot = (high[..., None] == jnp.arange(upper, dtype=jnp.int32)).astype(jnp.bfloat16)
        first = tile_values[..., None] * high_hot
        second = tile_weight[:, None, None] * high_hot
        stacked = jnp.concatenate([first, second, high_hot], axis=-1).reshape(count, 3 * upper)
        low_hot = (
            (low[..., None] == jnp.arange(lanes, dtype=jnp.int32))
            .astype(jnp.bfloat16)
            .reshape(count, lanes)
        )
        binned = lax.dot_general(
            stacked, low_hot, (((0,), (0,)), ((), ())), preferred_element_type=jnp.float32
        )
        return (total_map + select[:, None, None] * binned[None], None)

    start = jnp.zeros((spans, 3 * upper, lanes), jnp.float32)
    binned_map, unused = lax.scan(bin_tile, start, (values, where, weight_low, selector))
    binned_map = binned_map.reshape(spans, 3, BLOCK_PIX)
    count_det = lax.axis_size("det")
    count_sub = lax.axis_size("sub")
    peers = count_det * count_sub
    width = BLOCK_PIX // peers
    pieces = binned_map.reshape(spans, 3, peers, width)
    labels = jnp.broadcast_to(
        own_row.astype(jnp.float32)[:, None, None, None], (spans, 1, peers, 1)
    )
    received, got_labels = (
        lax.all_to_all(pieces, ("det", "sub"), split_axis=2, concat_axis=0, tiled=True),
        lax.all_to_all(labels, ("det", "sub"), split_axis=2, concat_axis=0, tiled=True),
    )
    received = received.reshape(peers * spans, 3 * width)
    got_labels = got_labels.reshape(peers * spans)
    placing = (got_labels[:, None] == jnp.arange(nblocks, dtype=jnp.float32)[None, :]).astype(
        jnp.float32
    )
    gathered = lax.dot_general(
        placing,
        received,
        (((0,), (0,)), ((), ())),
        precision=lax.Precision.HIGHEST,
        preferred_element_type=jnp.float32,
    )
    gathered = gathered.reshape(nblocks, 3, width)
    mine = lax.psum_scatter(gathered, "blk", scatter_dimension=0, tiled=True)
    signal_sum, weight_sum, hit_count = (mine[:, 0], mine[:, 1], mine[:, 2])
    return (signal_sum, weight_sum, hit_count)


def solution(mesh):
    placed = (
        P(("groups", "det"), None, ("blk", "sub")),
        P("groups", "det", ("blk", "sub")),
        P("groups", ("blk", "sub")),
        P("groups"),
        P("groups"),
    )
    return jax.shard_map(
        on_device,
        mesh=mesh,
        in_specs=placed,
        out_specs=(
            P(("groups", "blk"), ("det", "sub")),
            P(("groups", "blk"), ("det", "sub")),
            P(("groups", "blk"), ("det", "sub")),
        ),
        check_vma=False,
    )
```

profile of v0, /device:TPU:0, one launch (start us, length us, event | category | flops | bytes accessed | tf_op | source)
XLA Modules:
  0.0 50.1 jit_solution(9082960590155810975)
XLA Ops:
  0.6 1.6 %copy.35 = f32[32,4,256]{2,0,1:T(8,128)} copy(f32[32,4,256]{2,1,0:T(4,128)} %param.7) | data formatting | bytes 262144 | tf_op args[0]
  2.2 6.5 %all-to-all-start.1 = ((f32[32,4,256]{2,0,1:T(8,128)}), f32[32,4,256]{2,0,1:T(8,128)S(1)}, u32[]{:S(2)}, u32[]{:S(2)}) async-start(f32[32,4,256]{2,0,1:T(8,128)} %copy.35), calls=%async_computation.1 | async-start | bytes 262144 | tf_op jit(solution)/shard_map/all_to_all | solution.py:18
  8.7 0.7 %select_reduce_fusion = (f32[]{:T(128)}, f32[128]{0:T(128)S(1)}) fusion(f32[8]{0:T(128)S(1)} %copy-done.2, s32[128]{0:T(128)S(1)} %copy-done.3), kind=kLoop, calls=%fused_computation.40 | loop fusion | flops 3967 | bytes 1060 | tf_op jit(solution)/shard_map/reduce_sum | solution.py:17
  9.6 0.2 convert_reduce_fusion
  9.8 4.9 %all-to-all-done.1 = f32[32,4,256]{2,0,1:T(8,128)S(1)} async-done(((f32[32,4,256]{2,0,1:T(8,128)}), f32[32,4,256]{2,0,1:T(8,128)S(1)}, u32[]{:S(2)}, u32[]{:S(2)}) %all-to-all-start.1) | async-done | bytes 131104 | tf_op jit(solution)/shard_map/all_to_all | solution.py:18
  14.8 0.6 %broadcast_in_dim.8 = f32[2,1,8,1]{0,3,1,2:T(1,128)} broadcast(f32[2]{0:T(128)S(1)} %convert_reduce_fusion), dimensions={0} | broadcast | bytes 72 | tf_op jit(solution)/shard_map/broadcast_in_dim | solution.py:77
  15.3 3.3 %all-to-all-start = ((f32[2,1,8,1]{0,3,1,2:T(1,128)}), f32[2,1,8,1]{0,3,1,2:T(1,128)S(1)}, u32[]{:S(2)}, u32[]{:S(2)}) async-start(f32[2,1,8,1]{0,3,1,2:T(1,128)} %broadcast_in_dim.8), calls=%async_computation | async-start | bytes 8192 | tf_op jit(solution)/shard_map/all_to_all | solution.py:82
  18.8 0.7 %divide_bitcast_fusion = f32[2,128]{1,0:T(2,128)S(1)} fusion(f32[256]{0:T(256)S(1)} %fusion.17, f32[]{:T(128)} %get-tuple-element.105), kind=kLoop, calls=%fused_computation.48 | loop fusion | flops 256 | bytes 2052 | tf_op jit(solution)/shard_map/div | solution.py:19
  19.5 0.2 fusion.21
  19.7 9.3 %while.13 = (s32[]{:T(128)}, f32[2,72,128]{2,1,0:T(8,128)S(1)}, f32[8,2]{1,0:T(8,128)S(1)}, s32[8,32,128]{2,1,0:T(8,128)S(1)}, bf16[8,32,128]{2,1,0:T(8,128)(2,1...) while((s32[]{:T(128)}, f32[2,72,128]{2,1,0:T(8,128)S(1)}, f32[8,2]{1,0:T(8,128)S(1)}, ...), condition=%wide.region_4.5_spmd.clone, body=%wide.region_3.4_spmd.clone.sunk | while | flops 78440448 | bytes 1548619 | solution.py:70
  19.8 0.1 fusion.35
  20.0 0.8 %fusion.36 = f32[72,128]{1,0:T(8,128)S(1)} fusion(s32[32,128]{1,0:T(8,128)S(1)} %add_select_fusion.5, bf16[32,128,24]{1,2,0:T(8,128)(2,1)S(1)} %fusion.33, bf16[32,128,24]{1,2,0:T(8,128)(2,1)S(1)} %get-tuple-element.169, bf16[32,128,24]{1,2,0:T(8,128)(2,1)S(1)} %get-tuple-element.170), kind=kOutput, calls=%fused_computation.2.clone.1 | convolution fusion | flops 77791232 | bytes 643072 | tf_op jit(solution)/shard_map/while/body/eval_jaxpr/dot_general | solution.py:64
  21.0 0.1 fusion.35
  21.2 0.8 %fusion.36 = f32[72,128]{1,0:T(8,128)S(1)} fusion(s32[32,128]{1,0:T(8,128)S(1)} %add_select_fusion.5, bf16[32,128,24]{1,2,0:T(8,128)(2,1)S(1)} %fusion.33, bf16[32,128,24]{1,2,0:T(8,128)(2,1)S(1)} %get-tuple-element.169, bf16[32,128,24]{1,2,0:T(8,128)(2,1)S(1)} %get-tuple-element.170), kind=kOutput, calls=%fused_computation.2.clone.1 | convolution fusion | flops 77791232 | bytes 643072 | tf_op jit(solution)/shard_map/while/body/eval_jaxpr/dot_general | solution.py:64
  22.1 0.1 fusion.35
  22.3 0.8 %fusion.36 = f32[72,128]{1,0:T(8,128)S(1)} fusion(s32[32,128]{1,0:T(8,128)S(1)} %add_select_fusion.5, bf16[32,128,24]{1,2,0:T(8,128)(2,1)S(1)} %fusion.33, bf16[32,128,24]{1,2,0:T(8,128)(2,1)S(1)} %get-tuple-element.169, bf16[32,128,24]{1,2,0:T(8,128)(2,1)S(1)} %get-tuple-element.170), kind=kOutput, calls=%fused_computation.2.clone.1 | convolution fusion | flops 77791232 | bytes 643072 | tf_op jit(solution)/shard_map/while/body/eval_jaxpr/dot_general | solution.py:64
  23.3 0.1 fusion.35
  23.5 0.8 %fusion.36 = f32[72,128]{1,0:T(8,128)S(1)} fusion(s32[32,128]{1,0:T(8,128)S(1)} %add_select_fusion.5, bf16[32,128,24]{1,2,0:T(8,128)(2,1)S(1)} %fusion.33, bf16[32,128,24]{1,2,0:T(8,128)(2,1)S(1)} %get-tuple-element.169, bf16[32,128,24]{1,2,0:T(8,128)(2,1)S(1)} %get-tuple-element.170), kind=kOutput, calls=%fused_computation.2.clone.1 | convolution fusion | flops 77791232 | bytes 643072 | tf_op jit(solution)/shard_map/while/body/eval_jaxpr/dot_general | solution.py:64
  24.4 0.1 fusion.35
  24.6 0.8 %fusion.36 = f32[72,128]{1,0:T(8,128)S(1)} fusion(s32[32,128]{1,0:T(8,128)S(1)} %add_select_fusion.5, bf16[32,128,24]{1,2,0:T(8,128)(2,1)S(1)} %fusion.33, bf16[32,128,24]{1,2,0:T(8,128)(2,1)S(1)} %get-tuple-element.169, bf16[32,128,24]{1,2,0:T(8,128)(2,1)S(1)} %get-tuple-element.170), kind=kOutput, calls=%fused_computation.2.clone.1 | convolution fusion | flops 77791232 | bytes 643072 | tf_op jit(solution)/shard_map/while/body/eval_jaxpr/dot_general | solution.py:64
  25.8 0.8 %fusion.36 = f32[72,128]{1,0:T(8,128)S(1)} fusion(s32[32,128]{1,0:T(8,128)S(1)} %add_select_fusion.5, bf16[32,128,24]{1,2,0:T(8,128)(2,1)S(1)} %fusion.33, bf16[32,128,24]{1,2,0:T(8,128)(2,1)S(1)} %get-tuple-element.169, bf16[32,128,24]{1,2,0:T(8,128)(2,1)S(1)} %get-tuple-element.170), kind=kOutput, calls=%fused_computation.2.clone.1 | convolution fusion | flops 77791232 | bytes 643072 | tf_op jit(solution)/shard_map/while/body/eval_jaxpr/dot_general | solution.py:64
  26.7 0.1 fusion.35
  26.9 0.8 %fusion.36 = f32[72,128]{1,0:T(8,128)S(1)} fusion(s32[32,128]{1,0:T(8,128)S(1)} %add_select_fusion.5, bf16[32,128,24]{1,2,0:T(8,128)(2,1)S(1)} %fusion.33, bf16[32,128,24]{1,2,0:T(8,128)(2,1)S(1)} %get-tuple-element.169, bf16[32,128,24]{1,2,0:T(8,128)(2,1)S(1)} %get-tuple-element.170), kind=kOutput, calls=%fused_computation.2.clone.1 | convolution fusion | flops 77791232 | bytes 643072 | tf_op jit(solution)/shard_map/while/body/eval_jaxpr/dot_general | solution.py:64
  27.9 0.1 fusion.35
  28.1 0.8 %fusion.36 = f32[72,128]{1,0:T(8,128)S(1)} fusion(s32[32,128]{1,0:T(8,128)S(1)} %add_select_fusion.5, bf16[32,128,24]{1,2,0:T(8,128)(2,1)S(1)} %fusion.33, bf16[32,128,24]{1,2,0:T(8,128)(2,1)S(1)} %get-tuple-element.169, bf16[32,128,24]{1,2,0:T(8,128)(2,1)S(1)} %get-tuple-element.170), kind=kOutput, calls=%fused_computation.2.clone.1 | convolution fusion | flops 77791232 | bytes 643072 | tf_op jit(solution)/shard_map/while/body/eval_jaxpr/dot_general | solution.py:64
  29.0 0.7 %copy.37 = f32[2,3,8,384]{3,0,1,2:T(2,128)} copy(f32[2,3,8,384]{3,2,1,0:T(8,128)S(1)} %reshape_reshape.3) | data formatting | bytes 147456 | tf_op jit(solution)/shard_map/reshape;reshape | solution.py:76
  29.7 5.0 %all-to-all-start.2 = ((f32[2,3,8,384]{3,0,1,2:T(2,128)}), f32[2,3,8,384]{3,0,1,2:T(2,128)S(1)}, u32[]{:S(2)}, u32[]{:S(2)}) async-start(f32[2,3,8,384]{3,0,1,2:T(2,128)} %copy.37), calls=%async_computation.2 | async-start | bytes 147456 | tf_op jit(solution)/shard_map/all_to_all | solution.py:81
  34.7 0.6 %dynamic-slice = u32[1]{0:T(128)} dynamic-slice(u32[32]{0:T(128)S(1)} %copy-done.4, u32[]{:T(128)S(6)} %add.43), dynamic_slice_sizes={1} | dynamic-slice | bytes 12
  36.2 4.5 %all-to-all-done.2 = f32[2,3,8,384]{3,0,1,2:T(2,128)S(1)} async-done(((f32[2,3,8,384]{3,0,1,2:T(2,128)}), f32[2,3,8,384]{3,0,1,2:T(2,128)S(1)}, u32[]{:S(2)}, u32[]{:S(2)}) %all-to-all-start.2) | async-done | bytes 73760 | tf_op jit(solution)/shard_map/all_to_all | solution.py:81
  40.7 0.1 fusion.18
  40.9 8.6 %all-reduce = f32[8,3,384]{2,0,1:T(8,128)S(1)} all-reduce(f32[8,3,384]{2,0,1:T(8,128)S(1)} %fusion.18), channel_id=2, replica_groups=mesh['groups'=2,'det'=4,'blk'=2,'sub'=2] {'blk'}, use_global_device_ids=true, to_apply=%region_5.6.clone | all-reduce | flops 9216 | bytes 73728
  49.5 0.6 %dynamic-slice_bitcast_fusion.1 = (f32[4,384]{1,0:T(4,128)}, f32[4,384]{1,0:T(4,128)}, f32[4,384]{1,0:T(4,128)}) fusion(f32[8,3,384]{2,0,1:T(8,128)S(1)} %all-reduce, u32[]{:T(128)S(6)} %multiply.1, u32[]{:T(128)S(6)} %convert.1, u32[]{:T(128)S(6)} %convert), kind=kLoop, calls=%fused_computation.37 | loop fusion | bytes 36876 | tf_op jit(solution)/shard_map/squeeze | solution.py:98
  (84 shorter events, 2.4 us)
Async XLA Ops:
  2.2 6.5 %copy-start.2 = (f32[8]{0:T(128)S(1)}, f32[8]{0:T(128)}, u32[]{:S(2)}) copy-start(f32[8]{0:T(128)} %param.11) | copy-start | bytes 100
  2.2 6.5 %copy-start.3 = (s32[128]{0:T(128)S(1)}, s32[128]{0:T(128)}, u32[]{:S(2)}) copy-start(s32[128]{0:T(128)} %param.10) | copy-start | bytes 1540
  2.2 7.3 %copy-start = (s32[128,1,256]{2,1,0:T(1,128)S(1)}, s32[128,1,256]{2,1,0:T(1,128)}, u32[]{:S(2)}) copy-start(s32[128,1,256]{2,1,0:T(1,128)} %param.8) | copy-start | bytes 393220
  2.2 12.6 %all-to-all-start.1 = ((f32[32,4,256]{2,0,1:T(8,128)}), f32[32,4,256]{2,0,1:T(8,128)S(1)}, u32[]{:S(2)}, u32[]{:S(2)}) async-start(f32[32,4,256]{2,0,1:T(8,128)} %copy.35), calls=%async_computation.1 | async-start | bytes 262144 | tf_op jit(solution)/shard_map/all_to_all | solution.py:18
  8.7 0.9 %copy-start.1 = (s32[4,2]{0,1:T(2,128)S(1)}, s32[4,2]{0,1:T(2,128)}, u32[]{:S(2)}) copy-start(s32[4,2]{0,1:T(2,128)} %param.9) | copy-start | bytes 100
  15.3 14.3 %all-to-all-start = ((f32[2,1,8,1]{0,3,1,2:T(1,128)}), f32[2,1,8,1]{0,3,1,2:T(1,128)S(1)}, u32[]{:S(2)}, u32[]{:S(2)}) async-start(f32[2,1,8,1]{0,3,1,2:T(1,128)} %broadcast_in_dim.8), calls=%async_computation | async-start | bytes 8192 | tf_op jit(solution)/shard_map/all_to_all | solution.py:82
  29.0 5.7 %copy-start.4 = (u32[32]{0:T(128)S(1)}, u32[32]{0:T(128)}, u32[]{:S(2)}) copy-start(u32[32]{0:T(128)} %constant.84) | copy-start | bytes 388
  29.7 11.0 %all-to-all-start.2 = ((f32[2,3,8,384]{3,0,1,2:T(2,128)}), f32[2,3,8,384]{3,0,1,2:T(2,128)S(1)}, u32[]{:S(2)}, u32[]{:S(2)}) async-start(f32[2,3,8,384]{3,0,1,2:T(2,128)} %copy.37), calls=%async_computation.2 | async-start | bytes 147456 | tf_op jit(solution)/shard_map/all_to_all | solution.py:81
where the time goes:
time: 50.5 us; the launch traced here: 50.1 us
  starting transfers between devices  14.8 us (29%)
  waiting for transfers between devices  9.42 us (19%)
  blocking collectives  8.57 us (17%)
  matrix products  6.57 us (13%)
  local copies, waits for them, and re-layouts  4.85 us (10%)
  other arithmetic  4.02 us (8%)
  between operations  1.39 us (3%)
    unnamed x1, blocking collectives  8.57 us
    all_to_all x1, starting transfers between devices, on_device(): lax.all_to_all(tod, 'det', split_axis=1, concat_axis=0, tiled=True)  6.48 us
    dot_general x8, matrix products, bin_tile(): lax.dot_general(stacked, low_hot, (((0,), (0,)), ((), ())), preferred_ele...  6.42 us
    all_to_all x1, starting transfers between devices, on_device(): lax.all_to_all(pieces, ('det', 'sub'), split_axis=2, concat_axis=0, tiled...  5.03 us
    all_to_all x1, waiting for transfers between devices, on_device(): lax.all_to_all(tod, 'det', split_axis=1, concat_axis=0, tiled=True)  4.93 us
    all_to_all x1, waiting for transfers between devices, on_device(): lax.all_to_all(pieces, ('det', 'sub'), split_axis=2, concat_axis=0, tiled...  4.49 us
    all_to_all x1, starting transfers between devices, on_device(): lax.all_to_all(labels, ('det', 'sub'), split_axis=2, concat_axis=0, tiled...  3.31 us
    unnamed x12, local copies, waits for them, and re-layouts  2.17 us
  transfers between devices with their start and end apart: 3, of which 2 were waited for; matrix products, arithmetic and copies ran while one was open for 25% of the time, Pallas kernels for 0%

commit v1 on v0

--- a/solution.py
+++ b/solution.py
@@ -77,8 +77,17 @@
     labels = jnp.broadcast_to(
         own_row.astype(jnp.float32)[:, None, None, None], (spans, 1, peers, 1)
     )
+    report_pieces_all = lambda chunk, array_dim, d_out: jnp.concatenate(
+        lax.all_to_all(
+            jnp.stack(jnp.split(chunk, lax.axis_size(("det", "sub")), array_dim)),
+            axis_name=("det", "sub"),
+            split_axis=0,
+            concat_axis=0,
+        ),
+        axis=d_out,
+    )
     received, got_labels = (
-        lax.all_to_all(pieces, ("det", "sub"), split_axis=2, concat_axis=0, tiled=True),
+        report_pieces_all(pieces, 2, 0),
         lax.all_to_all(labels, ("det", "sub"), split_axis=2, concat_axis=0, tiled=True),
     )
     received = received.reshape(peers * spans, 3 * width)

time: 50.5 us -> 54.8 us (1.085)
  local copies, waits for them, and re-layouts: 4.85 us -> 8.97 us
    unnamed x12 -> x19, local copies, waits for them, and re-layouts: 2.17 us -> 6.38 us
    another operation x2 -> x1, local copies, waits for them, and re-layouts: 0.68 us -> 0.02 us  [on_device(): pieces = binned_map.reshape(spans, 3, peers, width)]
    another operation x0 -> x1, local copies, waits for them, and re-layouts: none -> 0.6 us  [on_device(): jnp.stack(jnp.split(chunk, lax.axis_size(('det', 'sub')), array_dim))]
  transfers between devices with their start and end apart: 3 -> 3, of which waited for: 2 -> 2; matrix products, arithmetic and copies ran while one was open for 25% -> 30% of each run, Pallas kernels for 0% -> 0%
where the time goes in v1:
time: 54.8 us; the launch traced here: 54.4 us
  starting transfers between devices  14.8 us (27%)
  waiting for transfers between devices  9.42 us (17%)
  local copies, waits for them, and re-layouts  8.97 us (16%)
  blocking collectives  8.59 us (16%)
  matrix products  6.57 us (12%)
  other arithmetic  4.21 us (8%)
  between operations  1.39 us (3%)
    unnamed x1, blocking collectives  8.59 us
    all_to_all x1, starting transfers between devices, on_device(): lax.all_to_all(tod, 'det', split_axis=1, concat_axis=0, tiled=True)  6.48 us
    dot_general x8, matrix products, bin_tile(): lax.dot_general(stacked, low_hot, (((0,), (0,)), ((), ())), preferred_ele...  6.42 us
    unnamed x19, local copies, waits for them, and re-layouts  6.38 us
    all_to_all x1, starting transfers between devices, on_device(): lax.all_to_all(jnp.stack(jnp.split(chunk, lax.axis_size(('det', 'sub')),...  5.03 us
    all_to_all x1, waiting for transfers between devices, on_device(): lax.all_to_all(tod, 'det', split_axis=1, concat_axis=0, tiled=True)  4.93 us
    all_to_all x1, waiting for transfers between devices, on_device(): lax.all_to_all(jnp.stack(jnp.split(chunk, lax.axis_size(('det', 'sub')),...  4.49 us
    all_to_all x1, starting transfers between devices, on_device(): lax.all_to_all(labels, ('det', 'sub'), split_axis=2, concat_axis=0, tiled...  3.31 us
  transfers between devices with their start and end apart: 3, of which 2 were waited for; matrix products, arithmetic and copies ran while one was open for 30% of the time, Pallas kernels for 0%

profile of v1, /device:TPU:0, one launch (start us, length us, event | category | flops | bytes accessed | tf_op | source)
XLA Modules:
  0.0 54.4 jit_solution(8419422077658927663)
XLA Ops:
  0.6 1.6 %copy.25 = f32[32,4,256]{2,0,1:T(8,128)} copy(f32[32,4,256]{2,1,0:T(4,128)} %param.7) | data formatting | bytes 262144 | tf_op args[0]
  2.2 6.5 %all-to-all-start.1 = ((f32[32,4,256]{2,0,1:T(8,128)}), f32[32,4,256]{2,0,1:T(8,128)S(1)}, u32[]{:S(2)}, u32[]{:S(2)}) async-start(f32[32,4,256]{2,0,1:T(8,128)} %copy.25), calls=%async_computation.1 | async-start | bytes 262144 | tf_op jit(solution)/shard_map/all_to_all | solution.py:18
  8.7 0.7 %select_reduce_fusion = (f32[]{:T(128)}, f32[128]{0:T(128)S(1)}) fusion(f32[8]{0:T(128)S(1)} %copy-done.2, s32[128]{0:T(128)S(1)} %copy-done.3), kind=kLoop, calls=%fused_computation.56 | loop fusion | flops 3967 | bytes 1060 | tf_op jit(solution)/shard_map/reduce_sum | solution.py:17
  9.6 0.2 convert_reduce_fusion
  9.8 4.9 %all-to-all-done.1 = f32[32,4,256]{2,0,1:T(8,128)S(1)} async-done(((f32[32,4,256]{2,0,1:T(8,128)}), f32[32,4,256]{2,0,1:T(8,128)S(1)}, u32[]{:S(2)}, u32[]{:S(2)}) %all-to-all-start.1) | async-done | bytes 131104 | tf_op jit(solution)/shard_map/all_to_all | solution.py:18
  14.8 0.6 %broadcast_in_dim.8 = f32[2,1,8,1]{0,3,1,2:T(1,128)} broadcast(f32[2]{0:T(128)S(1)} %convert_reduce_fusion), dimensions={0} | broadcast | bytes 72 | tf_op jit(solution)/shard_map/broadcast_in_dim | solution.py:77
  15.4 3.3 %all-to-all-start = ((f32[2,1,8,1]{0,3,1,2:T(1,128)}), f32[2,1,8,1]{0,3,1,2:T(1,128)S(1)}, u32[]{:S(2)}, u32[]{:S(2)}) async-start(f32[2,1,8,1]{0,3,1,2:T(1,128)} %broadcast_in_dim.8), calls=%async_computation | async-start | bytes 8192 | tf_op jit(solution)/shard_map/all_to_all | solution.py:91
  18.8 0.7 %divide_bitcast_fusion = f32[2,128]{1,0:T(2,128)S(1)} fusion(f32[256]{0:T(256)S(1)} %fusion.17, f32[]{:T(128)} %get-tuple-element.105), kind=kLoop, calls=%fused_computation.64 | loop fusion | flops 256 | bytes 2052 | tf_op jit(solution)/shard_map/div | solution.py:19
  19.5 0.2 fusion.21
  19.7 9.2 %while.13 = (s32[]{:T(128)}, f32[2,72,128]{2,1,0:T(8,128)S(1)}, f32[8,2]{1,0:T(8,128)S(1)}, s32[8,32,128]{2,1,0:T(8,128)S(1)}, bf16[8,32,128]{2,1,0:T(8,128)(2,1...) while((s32[]{:T(128)}, f32[2,72,128]{2,1,0:T(8,128)S(1)}, f32[8,2]{1,0:T(8,128)S(1)}, ...), condition=%wide.region_4.5_spmd.clone, body=%wide.region_3.4_spmd.clone.sunk | while | flops 78440448 | bytes 1548619 | solution.py:70
  20.0 0.8 %fusion.36 = f32[72,128]{1,0:T(8,128)S(1)} fusion(s32[32,128]{1,0:T(8,128)S(1)} %add_select_fusion.5, bf16[32,128,24]{1,2,0:T(8,128)(2,1)S(1)} %fusion.33, bf16[32,128,24]{1,2,0:T(8,128)(2,1)S(1)} %get-tuple-element.169, bf16[32,128,24]{1,2,0:T(8,128)(2,1)S(1)} %get-tuple-element.170), kind=kOutput, calls=%fused_computation.2.clone.1 | convolution fusion | flops 77791232 | bytes 643072 | tf_op jit(solution)/shard_map/while/body/eval_jaxpr/dot_general | solution.py:64
  21.2 0.8 %fusion.36 = f32[72,128]{1,0:T(8,128)S(1)} fusion(s32[32,128]{1,0:T(8,128)S(1)} %add_select_fusion.5, bf16[32,128,24]{1,2,0:T(8,128)(2,1)S(1)} %fusion.33, bf16[32,128,24]{1,2,0:T(8,128)(2,1)S(1)} %get-tuple-element.169, bf16[32,128,24]{1,2,0:T(8,128)(2,1)S(1)} %get-tuple-element.170), kind=kOutput, calls=%fused_computation.2.clone.1 | convolution fusion | flops 77791232 | bytes 643072 | tf_op jit(solution)/shard_map/while/body/eval_jaxpr/dot_general | solution.py:64
  22.3 0.8 %fusion.36 = f32[72,128]{1,0:T(8,128)S(1)} fusion(s32[32,128]{1,0:T(8,128)S(1)} %add_select_fusion.5, bf16[32,128,24]{1,2,0:T(8,128)(2,1)S(1)} %fusion.33, bf16[32,128,24]{1,2,0:T(8,128)(2,1)S(1)} %get-tuple-element.169, bf16[32,128,24]{1,2,0:T(8,128)(2,1)S(1)} %get-tuple-element.170), kind=kOutput, calls=%fused_computation.2.clone.1 | convolution fusion | flops 77791232 | bytes 643072 | tf_op jit(solution)/shard_map/while/body/eval_jaxpr/dot_general | solution.py:64
  23.5 0.8 %fusion.36 = f32[72,128]{1,0:T(8,128)S(1)} fusion(s32[32,128]{1,0:T(8,128)S(1)} %add_select_fusion.5, bf16[32,128,24]{1,2,0:T(8,128)(2,1)S(1)} %fusion.33, bf16[32,128,24]{1,2,0:T(8,128)(2,1)S(1)} %get-tuple-element.169, bf16[32,128,24]{1,2,0:T(8,128)(2,1)S(1)} %get-tuple-element.170), kind=kOutput, calls=%fused_computation.2.clone.1 | convolution fusion | flops 77791232 | bytes 643072 | tf_op jit(solution)/shard_map/while/body/eval_jaxpr/dot_general | solution.py:64
  24.6 0.8 %fusion.36 = f32[72,128]{1,0:T(8,128)S(1)} fusion(s32[32,128]{1,0:T(8,128)S(1)} %add_select_fusion.5, bf16[32,128,24]{1,2,0:T(8,128)(2,1)S(1)} %fusion.33, bf16[32,128,24]{1,2,0:T(8,128)(2,1)S(1)} %get-tuple-element.169, bf16[32,128,24]{1,2,0:T(8,128)(2,1)S(1)} %get-tuple-element.170), kind=kOutput, calls=%fused_computation.2.clone.1 | convolution fusion | flops 77791232 | bytes 643072 | tf_op jit(solution)/shard_map/while/body/eval_jaxpr/dot_general | solution.py:64
  25.8 0.8 %fusion.36 = f32[72,128]{1,0:T(8,128)S(1)} fusion(s32[32,128]{1,0:T(8,128)S(1)} %add_select_fusion.5, bf16[32,128,24]{1,2,0:T(8,128)(2,1)S(1)} %fusion.33, bf16[32,128,24]{1,2,0:T(8,128)(2,1)S(1)} %get-tuple-element.169, bf16[32,128,24]{1,2,0:T(8,128)(2,1)S(1)} %get-tuple-element.170), kind=kOutput, calls=%fused_computation.2.clone.1 | convolution fusion | flops 77791232 | bytes 643072 | tf_op jit(solution)/shard_map/while/body/eval_jaxpr/dot_general | solution.py:64
  26.9 0.8 %fusion.36 = f32[72,128]{1,0:T(8,128)S(1)} fusion(s32[32,128]{1,0:T(8,128)S(1)} %add_select_fusion.5, bf16[32,128,24]{1,2,0:T(8,128)(2,1)S(1)} %fusion.33, bf16[32,128,24]{1,2,0:T(8,128)(2,1)S(1)} %get-tuple-element.169, bf16[32,128,24]{1,2,0:T(8,128)(2,1)S(1)} %get-tuple-element.170), kind=kOutput, calls=%fused_computation.2.clone.1 | convolution fusion | flops 77791232 | bytes 643072 | tf_op jit(solution)/shard_map/while/body/eval_jaxpr/dot_general | solution.py:64
  28.1 0.8 %fusion.36 = f32[72,128]{1,0:T(8,128)S(1)} fusion(s32[32,128]{1,0:T(8,128)S(1)} %add_select_fusion.5, bf16[32,128,24]{1,2,0:T(8,128)(2,1)S(1)} %fusion.33, bf16[32,128,24]{1,2,0:T(8,128)(2,1)S(1)} %get-tuple-element.169, bf16[32,128,24]{1,2,0:T(8,128)(2,1)S(1)} %get-tuple-element.170), kind=kOutput, calls=%fused_computation.2.clone.1 | convolution fusion | flops 77791232 | bytes 643072 | tf_op jit(solution)/shard_map/while/body/eval_jaxpr/dot_general | solution.py:64
  29.0 0.6 %constant_dynamic-update-slice_fusion.7 = f32[8,2,3,1,384]{4,3,2,1,0:T(1,128)} fusion(f32[2,3,8,384]{3,2,1,0:T(8,128)S(1)} %reshape_reshape.6), kind=kLoop, calls=%fused_computation.44 | loop fusion | bytes 18432
  29.6 0.6 %constant_dynamic-update-slice_fusion.6 = f32[8,2,3,1,384]{4,3,2,1,0:T(1,128)} fusion(f32[8,2,3,1,384]{4,3,2,1,0:T(1,128)} %constant_dynamic-update-slice_fusion.7, f32[2,3,8,384]{3,2,1,0:T(8,128)S(1)} %reshape_reshape.6), kind=kLoop, calls=%fused_computation.43 | loop fusion | bytes 18432
  30.2 0.6 %constant_dynamic-update-slice_fusion.5 = f32[8,2,3,1,384]{4,3,2,1,0:T(1,128)} fusion(f32[8,2,3,1,384]{4,3,2,1,0:T(1,128)} %constant_dynamic-update-slice_fusion.6, f32[2,3,8,384]{3,2,1,0:T(8,128)S(1)} %reshape_reshape.6), kind=kLoop, calls=%fused_computation.42 | loop fusion | bytes 18432
  30.8 0.6 %constant_dynamic-update-slice_fusion.4 = f32[8,2,3,1,384]{4,3,2,1,0:T(1,128)} fusion(f32[8,2,3,1,384]{4,3,2,1,0:T(1,128)} %constant_dynamic-update-slice_fusion.5, f32[2,3,8,384]{3,2,1,0:T(8,128)S(1)} %reshape_reshape.6), kind=kLoop, calls=%fused_computation.41 | loop fusion | bytes 18432
  31.4 0.6 %constant_dynamic-update-slice_fusion.3 = f32[8,2,3,1,384]{4,3,2,1,0:T(1,128)} fusion(f32[8,2,3,1,384]{4,3,2,1,0:T(1,128)} %constant_dynamic-update-slice_fusion.4, f32[2,3,8,384]{3,2,1,0:T(8,128)S(1)} %reshape_reshape.6), kind=kLoop, calls=%fused_computation.40 | loop fusion | bytes 18432
  32.0 0.6 %constant_dynamic-update-slice_fusion.2 = f32[8,2,3,1,384]{4,3,2,1,0:T(1,128)} fusion(f32[8,2,3,1,384]{4,3,2,1,0:T(1,128)} %constant_dynamic-update-slice_fusion.3, f32[2,3,8,384]{3,2,1,0:T(8,128)S(1)} %reshape_reshape.6), kind=kLoop, calls=%fused_computation.39 | loop fusion | bytes 18432
  32.6 0.6 %constant_dynamic-update-slice_fusion.1 = f32[8,2,3,1,384]{4,3,2,1,0:T(1,128)} fusion(f32[8,2,3,1,384]{4,3,2,1,0:T(1,128)} %constant_dynamic-update-slice_fusion.2, f32[2,3,8,384]{3,2,1,0:T(8,128)S(1)} %reshape_reshape.6), kind=kLoop, calls=%fused_computation.38 | loop fusion | bytes 18432
  33.2 0.6 %constant_dynamic-update-slice_fusion = f32[8,2,3,1,384]{4,3,2,1,0:T(1,128)} fusion(f32[8,2,3,1,384]{4,3,2,1,0:T(1,128)} %constant_dynamic-update-slice_fusion.1, f32[2,3,8,384]{3,2,1,0:T(8,128)S(1)} %reshape_reshape.6), kind=kLoop, calls=%fused_computation.37 | loop fusion | bytes 18432 | tf_op jit(solution)/shard_map/stack | solution.py:82
  33.8 5.0 %all-to-all-start.2 = ((f32[8,2,3,1,384]{4,3,2,1,0:T(1,128)}), f32[8,2,3,1,384]{4,3,2,1,0:T(1,128)S(1)}, u32[]{:S(2)}, u32[]{:S(2)}) async-start(f32[8,2,3,1,384]{4,3,2,1,0:T(1,128)} %constant_dynamic-update-slice_fusion), calls=%async_computation.2 | async-start | bytes 147456 | tf_op jit(solution)/shard_map/all_to_all | solution.py:81
  38.9 0.6 %dynamic-slice = u32[1]{0:T(128)} dynamic-slice(u32[32]{0:T(128)S(1)} %copy-done.4, u32[]{:T(128)S(6)} %add.43), dynamic_slice_sizes={1} | dynamic-slice | bytes 12
  40.4 4.5 %all-to-all-done.2 = f32[8,2,3,1,384]{4,3,2,1,0:T(1,128)S(1)} async-done(((f32[8,2,3,1,384]{4,3,2,1,0:T(1,128)}), f32[8,2,3,1,384]{4,3,2,1,0:T(1,128)S(1)}, u32[]{:S(2)}, u32[]{:S(2)}) %all-to-all-start.2) | async-done | bytes 73760 | tf_op jit(solution)/shard_map/all_to_all | solution.py:81
  44.8 0.2 reduce.3
  45.2 8.6 %all-reduce = f32[8,3,384]{2,0,1:T(8,128)S(1)} all-reduce(f32[8,3,384]{2,0,1:T(8,128)S(1)} %fusion.18), channel_id=2, replica_groups=mesh['groups'=2,'det'=4,'blk'=2,'sub'=2] {'blk'}, use_global_device_ids=true, to_apply=%region_5.6.clone | all-reduce | flops 9216 | bytes 73728
  53.8 0.6 %dynamic-slice_bitcast_fusion.1 = (f32[4,384]{1,0:T(4,128)}, f32[4,384]{1,0:T(4,128)}, f32[4,384]{1,0:T(4,128)}) fusion(f32[8,3,384]{2,0,1:T(8,128)S(1)} %all-reduce, u32[]{:T(128)S(6)} %multiply.1, u32[]{:T(128)S(6)} %convert.1, u32[]{:T(128)S(6)} %convert), kind=kLoop, calls=%fused_computation.53 | loop fusion | bytes 36876 | tf_op jit(solution)/shard_map/squeeze | solution.py:107
  (91 shorter events, 3.3 us)
Async XLA Ops:
  2.2 6.5 %copy-start.2 = (f32[8]{0:T(128)S(1)}, f32[8]{0:T(128)}, u32[]{:S(2)}) copy-start(f32[8]{0:T(128)} %param.11) | copy-start | bytes 100
  2.2 6.5 %copy-start.3 = (s32[128]{0:T(128)S(1)}, s32[128]{0:T(128)}, u32[]{:S(2)}) copy-start(s32[128]{0:T(128)} %param.10) | copy-start | bytes 1540
  2.2 7.3 %copy-start = (s32[128,1,256]{2,1,0:T(1,128)S(1)}, s32[128,1,256]{2,1,0:T(1,128)}, u32[]{:S(2)}) copy-start(s32[128,1,256]{2,1,0:T(1,128)} %param.8) | copy-start | bytes 393220
  2.2 12.6 %all-to-all-start.1 = ((f32[32,4,256]{2,0,1:T(8,128)}), f32[32,4,256]{2,0,1:T(8,128)S(1)}, u32[]{:S(2)}, u32[]{:S(2)}) async-start(f32[32,4,256]{2,0,1:T(8,128)} %copy.25), calls=%async_computation.1 | async-start | bytes 262144 | tf_op jit(solution)/shard_map/all_to_all | solution.py:18
  8.7 0.9 %copy-start.1 = (s32[4,2]{0,1:T(2,128)S(1)}, s32[4,2]{0,1:T(2,128)}, u32[]{:S(2)}) copy-start(s32[4,2]{0,1:T(2,128)} %param.9) | copy-start | bytes 100
  15.4 18.5 %all-to-all-start = ((f32[2,1,8,1]{0,3,1,2:T(1,128)}), f32[2,1,8,1]{0,3,1,2:T(1,128)S(1)}, u32[]{:S(2)}, u32[]{:S(2)}) async-start(f32[2,1,8,1]{0,3,1,2:T(1,128)} %broadcast_in_dim.8), calls=%async_computation | async-start | bytes 8192 | tf_op jit(solution)/shard_map/all_to_all | solution.py:91
  29.0 9.9 %copy-start.4 = (u32[32]{0:T(128)S(1)}, u32[32]{0:T(128)}, u32[]{:S(2)}) copy-start(u32[32]{0:T(128)} %constant.84) | copy-start | bytes 388
  33.8 11.0 %all-to-all-start.2 = ((f32[8,2,3,1,384]{4,3,2,1,0:T(1,128)}), f32[8,2,3,1,384]{4,3,2,1,0:T(1,128)S(1)}, u32[]{:S(2)}, u32[]{:S(2)}) async-start(f32[8,2,3,1,384]{4,3,2,1,0:T(1,128)} %constant_dynamic-update-slice_fusion), calls=%async_computation.2 | async-start | bytes 147456 | tf_op jit(solution)/shard_map/all_to_all | solution.py:81
